TPU v7x, 32 devices: a whole 2x2x4 slice. The times are simulated.
32 devices in a mesh: dp: 16 (over z, x, core), head: 2 (over y).
Axes of the slice: x: 2, y: 2, z: 4, core: 2. Of those that a mesh axis runs over, the one named last changes fastest.
Arguments:
- tokens: bfloat16 [32768, 512], P(('dp', 'head')), may hold values from -6 to 6
- lengths: int32 [128], P('dp'), may hold values from 40 to 256, as said below
- ln1_gain: float32 [512], replicated, may hold values from 0.5 to 1.5
- ln1_bias: float32 [512], replicated, may hold values from -1 to 1
- w_query: bfloat16 [512, 512], P(None, 'head'), may hold values from -0.25 to 0.25
- w_key: bfloat16 [512, 512], P(None, 'head'), may hold values from -0.25 to 0.25
- w_value: bfloat16 [512, 512], P(None, 'head'), may hold values from -0.25 to 0.25
- w_out: bfloat16 [512, 512], P('head'), may hold values from -1 to 1
- sort_first: bfloat16 [512, 512], replicated, may hold values from -0.25 to 0.25
- sort_second: bfloat16 [512, 8], replicated, may hold values from -0.5 to 0.5
- ln2_gain: float32 [512], replicated, may hold values from 0.5 to 1.5
- ln2_bias: float32 [512], replicated, may hold values from -1 to 1
- w_up: bfloat16 [512, 2048], replicated, may hold values from -0.25 to 0.25
- w_down: bfloat16 [2048, 512], replicated, may hold values from -0.125 to 0.125
- cotangent: bfloat16 [32768, 512], P(('dp', 'head')), may hold values from -6 to 6
Outputs:
- output: bfloat16 [32768, 512], P(('dp', 'head'))
- input_grad: bfloat16 [32768, 512], P(('dp', 'head'))
- grad_ln1_gain: float32 [512], replicated
- grad_ln1_bias: float32 [512], replicated
- grad_query: float32 [512, 512], P(None, 'head')
- grad_key: float32 [512, 512], P(None, 'head')
- grad_value: float32 [512, 512], P(None, 'head')
- grad_out: float32 [512, 512], P('head')
- grad_sort_first: float32 [512, 512], replicated
- grad_sort_second: float32 [512, 8], replicated
- grad_ln2_gain: float32 [512], replicated
- grad_ln2_bias: float32 [512], replicated
- grad_up: float32 [512, 2048], replicated
- grad_down: float32 [2048, 512], replicated
Inputs may be any that keep to these rules, and one draw needn't show every extreme that they name: `lengths`: some sequence has exactly 256 valid tokens and some has exactly 40.
All inputs are finite; a program needn't handle non-finite values.
Results may differ from a plain program's by a relative error of at most 0.017.
Values may be sent and summed in bfloat16 or wider, within the bound.
No kernel may reach another device: no remote copies, remote signals or barrier semaphores. Data moves between devices by JAX's collectives and lax.ppermute only.
A program may use at most 192 MiB of HBM per device.

v0:
```python
import jax
import jax.numpy as jnp
from jax import lax
from jax.sharding import PartitionSpec as P

HD = 64
BL = 32
ITERS = 8
LMAX = 256
precise = lax.Precision.HIGHEST


def smooth_gate(values):
    return jax.nn.gelu(values, approximate=False)


def layer_norm(values, gain_vec, bias_vec):
    center = values - jnp.mean(values, axis=-1, keepdims=True)
    spread = jnp.mean(center * center, axis=-1, keepdims=True)
    return center * lax.rsqrt(spread + 1e-05) * gain_vec + bias_vec


def log_total(values, along):
    row_top = jnp.max(values, axis=along, keepdims=True)
    return row_top + jnp.log(jnp.sum(jnp.exp(values - row_top), axis=along, keepdims=True))


def sort_plan(summary, sort_one, sort_two, block_ok):
    hidden = smooth_gate(jnp.einsum("cid,de->cie", summary, sort_one, precision=precise))
    logits = jnp.einsum("cie,ej->cij", hidden, sort_two, precision=precise)
    diagonal = jnp.eye(logits.shape[1], dtype=jnp.bool_)[None]
    allowed = block_ok[:, :, None] & block_ok[:, None, :] | diagonal & ~block_ok[:, :, None]
    plan_log = jnp.where(allowed, logits, -1e30)
    for sweep_index in range(ITERS):
        plan_log = plan_log - log_total(plan_log, 2)
        plan_log = plan_log - log_total(plan_log, 1)
    return jnp.exp(plan_log)


def outer_product(left, right):
    return lax.dot_general(
        left, right, (((0,), (0,)), ((), ())), preferred_element_type=jnp.float32
    )


def attend_forward(queries, key_rows, value_rows, soft_plan, tok_ok, block_ok):
    tok_mask = tok_ok[..., None, None].astype(jnp.bfloat16)
    key_kept = key_rows * tok_mask
    value_kept = value_rows * tok_mask
    sorted_keys = jnp.einsum(
        "cij,cjthd->cithd", soft_plan, key_kept.astype(jnp.float32), precision=precise
    ).astype(jnp.bfloat16)
    sorted_values = jnp.einsum(
        "cij,cjthd->cithd", soft_plan, value_kept.astype(jnp.float32), precision=precise
    ).astype(jnp.bfloat16)
    all_keys = jnp.concatenate([key_kept, sorted_keys], axis=2)
    all_values = jnp.concatenate([value_kept, sorted_values], axis=2)
    score_scale = queries.shape[-1] ** (-0.5)
    scores = (
        jnp.einsum("cibhd,cikhd->cihbk", queries, all_keys, preferred_element_type=jnp.float32)
        * score_scale
    )
    key_ok = jnp.concatenate([tok_ok, jnp.broadcast_to(block_ok[:, :, None], tok_ok.shape)], axis=2)
    allowed = key_ok[:, :, None, None, :] | ~tok_ok[:, :, None, :, None]
    scores = jnp.where(allowed, scores, -1e30)
    weights = jnp.exp(scores - log_total(scores, 4))
    weights_low = weights.astype(jnp.bfloat16)
    mixed_rows = jnp.einsum(
        "cihbk,cikhd->cibhd", weights_low, all_values, preferred_element_type=jnp.float32
    )
    mixed_rows = mixed_rows * tok_ok[..., None, None].astype(jnp.float32)
    return (mixed_rows, (key_kept, all_keys, all_values, weights, weights_low))


def attend_backward(grad_mixed, queries, soft_plan, tok_ok, saved_state):
    key_kept, all_keys, all_values, weights, weights_low = saved_state
    block_len = key_kept.shape[2]
    score_scale = queries.shape[-1] ** (-0.5)
    value_kept = all_values[:, :, :block_len]
    grad_rows = grad_mixed * tok_ok[..., None, None].astype(jnp.bfloat16)
    grad_weights = jnp.einsum(
        "cibhd,cikhd->cihbk", grad_rows, all_values, preferred_element_type=jnp.float32
    )
    grad_all_values = jnp.einsum(
        "cihbk,cibhd->cikhd", weights_low, grad_rows, preferred_element_type=jnp.float32
    )
    weighted = jnp.sum(weights * grad_weights, axis=4, keepdims=True)
    grad_scores = (weights * (grad_weights - weighted)).astype(jnp.bfloat16)
    grad_queries = (
        jnp.einsum("cihbk,cikhd->cibhd", grad_scores, all_keys, preferred_element_type=jnp.float32)
        * score_scale
    )
    grad_all_keys = (
        jnp.einsum("cihbk,cibhd->cikhd", grad_scores, queries, preferred_element_type=jnp.float32)
        * score_scale
    )
    grad_sorted_keys = grad_all_keys[:, :, block_len:]
    grad_sorted_values = grad_all_values[:, :, block_len:]
    grad_plan = jnp.einsum(
        "cithd,cjthd->cij", grad_sorted_keys, key_kept.astype(jnp.float32), precision=precise
    )
    grad_plan = grad_plan + jnp.einsum(
        "cithd,cjthd->cij", grad_sorted_values, value_kept.astype(jnp.float32), precision=precise
    )
    key_total = grad_all_keys[:, :, :block_len] + jnp.einsum(
        "cij,cithd->cjthd", soft_plan, grad_sorted_keys, precision=precise
    )
    value_total = grad_all_values[:, :, :block_len] + jnp.einsum(
        "cij,cithd->cjthd", soft_plan, grad_sorted_values, precision=precise
    )
    tok_mask = tok_ok[..., None, None].astype(jnp.float32)
    return (
        grad_queries.astype(jnp.bfloat16),
        (key_total * tok_mask).astype(jnp.bfloat16),
        (value_total * tok_mask).astype(jnp.bfloat16),
        grad_plan,
    )


def run_attention(normed_here, span_list, query_cols, key_cols, value_cols, sort_one, sort_two):
    seq_count = span_list.shape[0]
    nblocks = LMAX // BL
    heads_here = query_cols.shape[1] // HD
    positions = jnp.arange(LMAX, dtype=jnp.int32)
    tok_ok = (positions[None, :] < span_list[:, None]).reshape(seq_count, nblocks, BL)
    block_ok = (jnp.arange(nblocks, dtype=jnp.int32) * BL)[None, :] < span_list[:, None]
    block_shape = (seq_count, nblocks, BL, heads_here, HD)
    queries = (
        jnp.dot(normed_here, query_cols, preferred_element_type=jnp.float32)
        .astype(jnp.bfloat16)
        .reshape(block_shape)
    )
    key_rows = (
        jnp.dot(normed_here, key_cols, preferred_element_type=jnp.float32)
        .astype(jnp.bfloat16)
        .reshape(block_shape)
    )
    value_rows = (
        jnp.dot(normed_here, value_cols, preferred_element_type=jnp.float32)
        .astype(jnp.bfloat16)
        .reshape(block_shape)
    )
    summary = jnp.sum(
        normed_here.reshape(seq_count, nblocks, BL, -1).astype(jnp.float32) * tok_ok[..., None],
        axis=2,
    ) * BL ** (-0.5)

    def plan_of(summary_in, first_in, second_in):
        return sort_plan(summary_in, first_in, second_in, block_ok)

    soft_plan, plan_back = jax.vjp(plan_of, summary, sort_one, sort_two)
    mixed_rows, saved_state = attend_forward(
        queries, key_rows, value_rows, soft_plan, tok_ok, block_ok
    )
    mixed_rows = mixed_rows.reshape(normed_here.shape[0], -1).astype(jnp.bfloat16)
    return (mixed_rows, queries, tok_ok, soft_plan, plan_back, saved_state)


def on_device(
    tokens,
    lengths,
    ln1_gain,
    ln1_bias,
    w_query,
    w_key,
    w_value,
    w_out,
    sort_first,
    sort_second,
    ln2_gain,
    ln2_bias,
    w_up,
    w_down,
    cotangent,
):
    head_side = lax.axis_index("head")
    local_rows = tokens.shape[0]
    inputs = tokens.astype(jnp.float32)
    sort_one = sort_first.astype(jnp.float32)
    sort_two = sort_second.astype(jnp.float32)
    normed_f, norm_back = jax.vjp(layer_norm, inputs, ln1_gain, ln1_bias)
    normed = normed_f.astype(jnp.bfloat16)
    normed_here = lax.all_gather(normed, "head", axis=0, tiled=True)
    query_cols, key_cols, value_cols, out_rows = (w_query, w_key, w_value, w_out)
    sort_share = (head_side == 0).astype(jnp.float32)
    mixed_rows, queries, tok_ok, soft_plan, plan_back, saved_state = run_attention(
        normed_here, lengths, query_cols, key_cols, value_cols, sort_one, sort_two
    )
    attention = lax.psum_scatter(
        jnp.dot(mixed_rows, w_out, preferred_element_type=jnp.float32).astype(jnp.bfloat16),
        "head",
        scatter_dimension=0,
        tiled=True,
    ).astype(jnp.float32)
    middle = inputs + attention
    normed_two_f, norm_two_back = jax.vjp(layer_norm, middle, ln2_gain, ln2_bias)
    normed_two = normed_two_f.astype(jnp.bfloat16)
    up_value = jnp.dot(normed_two, w_up, preferred_element_type=jnp.float32)
    hidden_f, gate_back = jax.vjp(smooth_gate, up_value)
    hidden = hidden_f.astype(jnp.bfloat16)
    output = (middle + jnp.dot(hidden, w_down, preferred_element_type=jnp.float32)).astype(
        jnp.bfloat16
    )
    grad_hidden = jnp.dot(cotangent, w_down.T, preferred_element_type=jnp.float32).astype(
        jnp.bfloat16
    )
    grad_upin = gate_back(grad_hidden.astype(jnp.float32))[0].astype(jnp.bfloat16)
    grad_down = outer_product(hidden, cotangent)
    grad_up = outer_product(normed_two, grad_upin)
    grad_middle_norm, grad_gain_two, grad_bias_two = norm_two_back(
        jnp.dot(grad_upin, w_up.T, preferred_element_type=jnp.float32)
    )
    grad_middle = cotangent.astype(jnp.float32) + grad_middle_norm
    grad_attention = grad_middle.astype(jnp.bfloat16)
    grad_attention_here = lax.all_gather(grad_attention, "head", axis=0, tiled=True)
    grad_w_out = outer_product(mixed_rows, grad_attention_here)
    grad_mixed = jnp.dot(
        grad_attention_here, out_rows.T, preferred_element_type=jnp.float32
    ).astype(jnp.bfloat16)
    grad_queries, grad_keys, grad_values, grad_plan = attend_backward(
        grad_mixed.reshape(queries.shape), queries, soft_plan, tok_ok, saved_state
    )
    grad_plan = lax.psum(grad_plan, "head")
    grad_summary, grad_first, grad_second = plan_back(grad_plan)
    rows_here = normed_here.shape[0]
    grad_queries = grad_queries.reshape(rows_here, -1)
    grad_keys = grad_keys.reshape(rows_here, -1)
    grad_values = grad_values.reshape(rows_here, -1)
    grad_spread = (grad_summary[:, :, None, :] * tok_ok[..., None] * BL ** (-0.5)).reshape(
        rows_here, -1
    )
    grad_w_query = outer_product(normed_here, grad_queries)
    grad_w_key = outer_product(normed_here, grad_keys)
    grad_w_value = outer_product(normed_here, grad_values)
    total_term = jnp.dot(grad_queries, w_query.T, preferred_element_type=jnp.float32)
    total_term = total_term + jnp.dot(grad_keys, w_key.T, preferred_element_type=jnp.float32)
    grad_normed = lax.psum_scatter(
        (total_term + jnp.dot(grad_values, w_value.T, preferred_element_type=jnp.float32)).astype(
            jnp.bfloat16
        ),
        "head",
        scatter_dimension=0,
        tiled=True,
    ).astype(jnp.float32)
    grad_normed = grad_normed + lax.dynamic_slice_in_dim(
        grad_spread, head_side * local_rows, local_rows, 0
    )
    grad_w_query, grad_w_key, grad_w_value, grad_w_out = lax.psum(
        (grad_w_query, grad_w_key, grad_w_value, grad_w_out), "dp"
    )
    grad_inputs_norm, grad_gain_one, grad_bias_one = norm_back(grad_normed)
    input_grad = (grad_middle + grad_inputs_norm).astype(jnp.bfloat16)
    summed = lax.psum(
        (
            grad_gain_one,
            grad_bias_one,
            grad_first * sort_share,
            grad_second * sort_share,
            grad_gain_two,
            grad_bias_two,
            grad_up,
            grad_down,
        ),
        ("dp", "head"),
    )
    return (
        output,
        input_grad,
        summed[0],
        summed[1],
        grad_w_query,
        grad_w_key,
        grad_w_value,
        grad_w_out,
        summed[2],
        summed[3],
        summed[4],
        summed[5],
        summed[6],
        summed[7],
    )


def solution(mesh):
    return jax.shard_map(
        on_device,
        mesh=mesh,
        in_specs=(
            P(("dp", "head"), None),
            P("dp"),
            P(),
            P(),
            P(None, "head"),
            P(None, "head"),
            P(None, "head"),
            P("head", None),
            P(),
            P(),
            P(),
            P(),
            P(),
            P(),
            P(("dp", "head"), None),
        ),
        out_specs=(
            P(("dp", "head"), None),
            P(("dp", "head"), None),
            P(),
            P(),
            P(None, "head"),
            P(None, "head"),
            P(None, "head"),
            P("head", None),
            P(),
            P(),
            P(),
            P(),
            P(),
            P(),
        ),
        check_vma=False,
    )
```

profile of v0, /device:TPU:0, one launch (start us, length us, event | category | flops | bytes accessed | tf_op | source)
XLA Modules:
  0.0 688.6 jit_solution(9410272883061867089)
XLA Ops:
  10.6 2.7 fusion.43
  16.0 33.3 %all-gather.3.cloned.1.call-done = bf16[2048,512]{1,0:T(8,128)(2,1)} async-done(((bf16[1024,512]{1,0:T(8,128)(2,1)}), bf16[2048,512]{1,0:T(8,128)(2,1)}) %all-gather.3.cloned.1.call-update) | async-done | bytes 2097168 | tf_op jit(solution)/shard_map/all_gather | solution.py:183
  49.3 2.9 fusion.17
  67.7 2.7 convolution_convert_fusion.2
  70.4 4.6 reshape.615
  75.0 3.3 convolution_convert_fusion.3
  78.3 4.4 reshape.614
  82.7 2.3 convolution_convert_fusion.4
  85.0 1.8 reshape.613
  86.8 4.9 copy_multiply_fusion.1
  91.7 1.9 convolution_convert_fusion.5
  93.6 1.9 convolution_convert_fusion.6
  95.5 1.9 pad_maximum_fusion
  97.4 2.5 fusion.34
  99.9 2.4 exponential_reduce_fusion
  102.4 2.5 fusion.47
  105.0 2.4 copy.60
  107.4 4.4 convert_element_type.198
  111.8 3.3 convolution_convert_fusion
  115.2 31.9 %reduce-scatter.3.cloned.1.call-done = bf16[1024,512]{1,0:T(8,128)(2,1)} async-done(((bf16[2048,512]{1,0:T(8,128)(2,1)}), bf16[1024,512]{1,0:T(8,128)(2,1)}) %reduce-scatter.3.cloned.1.call-update) | async-done | bytes 1048592 | tf_op jit(solution)/shard_map/reduce_scatter | solution.py:189
  148.7 1.7 multiply_reduce_fusion.3
  150.6 23.5 %multiply_convert_fusion = (bf16[1024,2048]{1,0:T(8,128)(2,1)}, f32[1024,2048]{1,0:T(8,128)S(1)}, f32[1024,2048]{1,0:T(8,128)}) fusion(bf16[512,2048]{1,0:T(8,128)(2,1)S(1)} %copy-done, bf16[1024,512]{1,0:T(8,128)(2,1)S(1)} %copy-done.26, bf16[1024,512]{1,0:T(8,128)(2,1)S(1)} %copy-done.2, f32[512]{0:T(512)} %param.26, f32[512]{0:T(512)} %param.25, ...), kind=kOutput, calls=%fused_computation.12 | convolution fusion | flops 2287992832 | bytes 25178112 | tf_op jit(solution)/shard_map/dot_general | solution.py:198
  174.0 6.9 %fusion.5 = bf16[1024,2048]{1,0:T(8,128)(2,1)S(1)} fusion(f32[1024,2048]{1,0:T(8,128)S(1)} %get-tuple-element.86, f32[1024,2048]{1,0:T(8,128)} %get-tuple-element.110, bf16[1024,512]{1,0:T(8,128)(2,1)S(1)} %copy-done.36, bf16[2048,512]{1,0:T(8,128)(2,1)S(1)} %copy-done.156), kind=kOutput, calls=%fused_computation.8 | convolution fusion | flops 2181038080 | bytes 24117248 | tf_op jit(solution)/shard_map/dot_general | solution.py:204
  180.9 3.3 multiply_reduce_fusion.1
  187.3 6.9 %fusion.167 = f32[2048,512]{1,0:T(8,128)} fusion(bf16[1024,2048]{1,0:T(8,128)(2,1)} %get-tuple-element.85, bf16[1024,512]{1,0:T(8,128)(2,1)} %param.29), kind=kOutput, calls=%fused_computation.381 | convolution fusion | flops 2147483648 | bytes 9437184 | tf_op jit(solution)/shard_map/dot_general | solution.py:41
  194.3 4.6 fusion.143
  198.9 21.4 %all-gather.5.cloned.1.call-done = bf16[2048,512]{1,0:T(8,128)(2,1)} async-done(((bf16[1024,512]{1,0:T(8,128)(2,1)}), bf16[2048,512]{1,0:T(8,128)(2,1)}) %all-gather.5.cloned.1.call-update) | async-done | bytes 2097168 | tf_op jit(solution)/shard_map/all_gather | solution.py:215
  220.3 2.3 convolution_convert_fusion.1
  222.6 1.8 reshape.616
  224.4 3.0 copy_multiply_fusion
  227.5 7.2 %multiply_reduce_fusion = (f32[8,8,4,32]{3,2,1,0:T(4,128)S(1)}, f32[8,8,4,32,64]{4,3,2,1,0:T(8,128)S(1)}) fusion(f32[8,8,4,32,64]{4,3,2,1,0:T(8,128)S(1)} %copy-done.4, f32[8,8,4,32]{3,2,1,0:T(4,128)} %bitcast.104, pred[8,8,32,64]{3,2,1,0:T(8,128)(4,1)S(1)} %broadcast_or_fusion, bf16[8,8,64,4,64]{4,1,3,2,0:T(8,128)(2,1)} %copy-done.35, ...), kind=kOutput, calls=%fused_computation.47 | convolution fusion | flops 69722112 | bytes 7536640 | tf_op jit(solution)/shard_map/cibhd,cikhd->cihbk/dot_general | solution.py:81
  234.7 5.8 convolution_bitcast_fusion
  240.5 2.7 multiply_convert_fusion.2
  246.7 3.1 copy-done.7
  249.8 6.4 fusion.65
  256.2 7.6 %fusion.24 = f32[8,8,32,4,64]{4,1,3,2,0:T(8,128)} fusion(f32[8,8,32,4,64]{4,2,3,1,0:T(8,128)S(1)} %slice.17, f32[8,8,8]{2,1,0:T(8,128)S(1)} %get-tuple-element.88, f32[8,8]{1,0:T(8,128)S(1)} %log_add_fusion.1, f32[8,8]{1,0:T(8,128)S(1)} %log_add_fusion.2), kind=kOutput, calls=%fused_computation.42 | convolution fusion | flops 50332672 | bytes 4196864 | tf_op jit(solution)/shard_map/cij,cithd->cjthd/dot_general | solution.py:105
  263.8 2.4 copy.65
  266.2 3.5 reshape.617
  269.7 2.7 fusion.161
  272.4 3.0 slice.19
  275.5 7.2 %fusion.22 = f32[8,8,32,4,64]{4,1,3,2,0:T(8,128)} fusion(f32[8,8,32,4,64]{4,2,3,1,0:T(8,128)S(1)} %slice.19, f32[8,8,8]{2,1,0:T(8,128)S(1)} %get-tuple-element.88, f32[8,8]{1,0:T(8,128)S(1)} %log_add_fusion.1, f32[8,8]{1,0:T(8,128)S(1)} %log_add_fusion.2), kind=kOutput, calls=%fused_computation.40 | convolution fusion | flops 50332672 | bytes 4196864 | tf_op jit(solution)/shard_map/cij,cithd->cjthd/dot_general | solution.py:108
  282.6 5.5 fusion.75
  288.2 7.2 %psum.91 = f32[8,8,8]{2,1,0:T(8,128)S(1)} all-reduce(f32[8,8,8]{2,1,0:T(8,128)S(1)} %fusion.75), channel_id=1, replica_groups=mesh['dp'=16,'head'=2] {'head'}, use_global_device_ids=true, to_apply=%region_44.45 | all-reduce | flops 512 | bytes 4096 | tf_op jit(solution)/shard_map/psum | solution.py:223
  295.4 12.7 %fusion.14 = (bf16[8,8,32,4,64]{4,2,3,1,0:T(8,128)(2,1)S(1)}, bf16[8,8,32,4,64]{4,2,3,1,0:T(8,128)(2,1)}) fusion(f32[8,8,64,4,64]{4,2,3,1,0:T(8,128)} %convolution_bitcast_fusion, f32[8,8,32,4,64]{4,1,3,2,0:T(8,128)} %fusion.22, f32[8,8,32]{2,1,0:T(8,128)S(1)} %get-tuple-element.101, f32[8,8,32,4,64]{4,1,3,2,0:T(8,128)} %fusion.24, ...), kind=kLoop, calls=%fused_computation.28 | loop fusion | flops 3145728 | bytes 10493952 | tf_op jit(solution)/shard_map/convert_element_type | solution.py:115
  308.4 2.5 copy.75
  310.9 3.5 reshape.619
  318.3 4.1 copy.70
  322.4 3.7 reshape.618
  328.8 2.1 add_convert_fusion
  332.3 3.4 fusion.166
  341.8 2.9 fusion.63
  346.0 6.3 add_convert_fusion.2
  354.0 10.0 %reduce-scatter.5.cloned.1.call-done = bf16[1024,512]{1,0:T(8,128)(2,1)} async-done(((bf16[2048,512]{1,0:T(8,128)(2,1)}), bf16[1024,512]{1,0:T(8,128)(2,1)}) %reduce-scatter.5.cloned.1.call-update) | async-done | bytes 1048592 | tf_op jit(solution)/shard_map/reduce_scatter | solution.py:237
  367.6 40.3 %all-reduce = (f32[512]{0:T(512)}, f32[512]{0:T(512)}, f32[512,8]{0,1:T(8,128)}, f32[512]{0:T(512)}, f32[512]{0:T(512)}) all-reduce(f32[512]{0:T(512)S(1)} %get-tuple-element.16, f32[512]{0:T(512)S(1)} %get-tuple-element.19, f32[512,8]{0,1:T(8,128)S(1)} %fusion.80, ...), channel_id=1, replica_groups=mesh['dp'=16,'head'=2] {'dp','head'}, use_global_device_ids=true, to_apply=%region_96.97 | all-reduce | flops 6144 | bytes 49152 | tf_op jit(solution)/shard_map/psum | solution.py:253
  407.9 3.2 add_convert_fusion.1
  411.1 55.9 %all-reduce.8.cloned.1.call-done = (f32[512,256]{1,0:T(8,128)}, f32[512,256]{1,0:T(8,128)}, f32[512,256]{1,0:T(8,128)}, f32[256,512]{1,0:T(8,128)}) async-done(((f32[512,256]{1,0:T(8,128)}, f32[512,256]{1,0:T(8,128)}, f32[512,256]{1,0:T(8,128)}, f32[256,512]{1,0:T(8,128)}), (f32[512,256]{1,0:T(8,128)}, f32[512,256]{1,0:T(8,128)}, f32[512,256]{1,0:T(8,128)}, ...) | async-done | bytes 2097168 | tf_op jit(solution)/shard_map/psum | solution.py:248
  467.0 198.9 %all-reduce.6.cloned.1.call-done = (f32[512,512]{1,0:T(8,128)}, f32[512,2048]{1,0:T(8,128)}, f32[2048,512]{1,0:T(8,128)}) async-done(((f32[512,512]{1,0:T(8,128)}, f32[512,2048]{1,0:T(8,128)}, f32[2048,512]{1,0:T(8,128)}), (f32[512,512]{1,0:T(8,128)}, f32[512,2048]{1,0:T(8,128)}, f32[2048,512]{1,0:T(8,128)})) %all-reduce.6.cloned.1.call-update) | async-done | bytes 9437200 | tf_op jit(solution)/shard_map/psum | solution.py:253
  665.9 2.0 copy.155
  668.0 1.9 copy.156
  669.8 1.9 copy.157
  671.7 1.9 copy.158
  673.6 2.3 copy.159
  675.8 2.1 copy.160
  679.5 2.0 copy.161
  (484 shorter events, 50.4 us)
Async XLA Ops:
  7.2 143.3 %copy-start = (bf16[512,2048]{1,0:T(8,128)(2,1)S(1)}, bf16[512,2048]{1,0:T(8,128)(2,1)}, u32[]{:S(2)}) copy-start(bf16[512,2048]{1,0:T(8,128)(2,1)} %param.27) | copy-start | bytes 6291460
  7.2 45.0 %copy-start.50 = (bf16[512,512]{1,0:T(8,128)(2,1)S(1)}, bf16[512,512]{1,0:T(8,128)(2,1)}, u32[]{:S(2)}) copy-start(bf16[512,512]{1,0:T(8,128)(2,1)} %param.23) | copy-start | bytes 1572868
  7.2 42.1 %all-gather.3.cloned.1.call-start = ((), (), s32[]{:S(2)}) async-start(), calls=%async_computation.2 | async-start | bytes 3145728 | tf_op jit(solution)/shard_map/all_gather | solution.py:183
  8.9 44.3 %copy-start.149 = (bf16[512,8]{0,1:T(8,128)(2,1)S(1)}, bf16[512,8]{0,1:T(8,128)(2,1)}, u32[]{:S(2)}) copy-start(bf16[512,8]{0,1:T(8,128)(2,1)} %param.24) | copy-start | bytes 24580
  8.9 40.4 %copy-start.68 = (f32[1024]{0:T(1024)}, f32[1024]{0:T(1024)S(1)}, u32[]{:S(2)}) copy-start(f32[1024]{0:T(1024)S(1)} %broadcast_multiply_fusion.1) | copy-start | bytes 12292
  10.6 38.7 %copy-start.111 = (f32[1024]{0:T(1024)}, f32[1024]{0:T(1024)S(1)}, u32[]{:S(2)}) copy-start(f32[1024]{0:T(1024)S(1)} %fusion.45) | copy-start | bytes 12292
  10.6 38.7 %copy-start.107 = (f32[1024]{0:T(1024)}, f32[1024]{0:T(1024)S(1)}, u32[]{:S(2)}) copy-start(f32[1024]{0:T(1024)S(1)} %fusion.127) | copy-start | bytes 12292
  13.3 133.8 %reduce-scatter.3.cloned.1.call-start = ((), (), s32[]{:S(2)}) async-start(), calls=%async_computation.3 | async-start | bytes 3145728 | tf_op jit(solution)/shard_map/reduce_scatter | solution.py:189
  13.5 281.9 %copy-start.48 = (f32[8,8,32]{2,1,0:T(8,128)}, f32[8,8,32]{2,1,0:T(8,128)S(1)}, u32[]{:S(2)}) copy-start(f32[8,8,32]{2,1,0:T(8,128)S(1)} %get-tuple-element.101) | copy-start | bytes 24580
  49.3 18.4 %copy-start.5 = (bf16[2048,512]{1,0:T(8,128)(2,1)S(1)}, bf16[2048,512]{1,0:T(8,128)(2,1)}, u32[]{:S(2)}) copy-start(bf16[2048,512]{1,0:T(8,128)(2,1)} %all-gather.3.cloned.1.call-done) | copy-start | bytes 6291460
  52.6 22.3 %copy-start.52 = (f32[8,8,512]{2,1,0:T(8,128)}, f32[8,8,512]{2,1,0:T(8,128)S(1)}, u32[]{:S(2)}) copy-start(f32[8,8,512]{2,1,0:T(8,128)S(1)} %get-tuple-element.105) | copy-start | bytes 393220
  53.1 21.9 %copy-start.54 = (f32[8,8,512]{2,1,0:T(8,128)}, f32[8,8,512]{2,1,0:T(8,128)S(1)}, u32[]{:S(2)}) copy-start(f32[8,8,512]{2,1,0:T(8,128)S(1)} %fusion.85) | copy-start | bytes 393220
  54.9 8.0 %copy-start.42 = (f32[8,8]{1,0:T(8,128)}, f32[8,8]{1,0:T(8,128)S(1)}, u32[]{:S(2)}) copy-start(f32[8,8]{1,0:T(8,128)S(1)} %log_add_fusion.16) | copy-start | bytes 772
  55.6 10.2 %copy-start.56 = (f32[8,8]{1,0:T(8,128)}, f32[8,8]{1,0:T(8,128)S(1)}, u32[]{:S(2)}) copy-start(f32[8,8]{1,0:T(8,128)S(1)} %log_add_fusion.15) | copy-start | bytes 772
  58.0 16.9 %copy-start.20 = (f32[8,8,8]{2,1,0:T(8,128)}, f32[8,8,8]{2,1,0:T(8,128)S(1)}, u32[]{:S(2)}) copy-start(f32[8,8,8]{2,1,0:T(8,128)S(1)} %get-tuple-element.94) | copy-start | bytes 6148
  61.0 14.0 %copy-start.22 = (f32[8,8,8]{2,1,0:T(8,128)}, f32[8,8,8]{2,1,0:T(8,128)S(1)}, u32[]{:S(2)}) copy-start(f32[8,8,8]{2,1,0:T(8,128)S(1)} %get-tuple-element.92) | copy-start | bytes 6148
  61.6 13.4 %copy-start.46 = (f32[8,8]{1,0:T(8,128)}, f32[8,8]{1,0:T(8,128)S(1)}, u32[]{:S(2)}) copy-start(f32[8,8]{1,0:T(8,128)S(1)} %log_add_fusion.8) | copy-start | bytes 772
  63.6 11.4 %copy-start.37 = (f32[8,8,8]{2,1,0:T(8,128)}, f32[8,8,8]{2,1,0:T(8,128)S(1)}, u32[]{:S(2)}) copy-start(f32[8,8,8]{2,1,0:T(8,128)S(1)} %get-tuple-element.90) | copy-start | bytes 6148
  67.7 7.3 %copy-start.62 = (bf16[512,256]{1,0:T(8,128)(2,1)S(1)}, bf16[512,256]{1,0:T(8,128)(2,1)}, u32[]{:S(2)}) copy-start(bf16[512,256]{1,0:T(8,128)(2,1)} %param.19) | copy-start | bytes 786436
  107.4 39.7 %copy-start.2 = (bf16[1024,512]{1,0:T(8,128)(2,1)S(1)}, bf16[1024,512]{1,0:T(8,128)(2,1)}, u32[]{:S(2)}) copy-start(bf16[1024,512]{1,0:T(8,128)(2,1)} %param.15) | copy-start | bytes 3145732
  115.1 105.2 %all-gather.5.cloned.1.call-start = ((), (), s32[]{:S(2)}) async-start(), calls=%async_computation.4 | async-start | bytes 3145728 | tf_op jit(solution)/shard_map/all_gather | solution.py:215
  150.5 33.8 %copy-start.147 = (f32[1024]{0:T(1024)}, f32[1024]{0:T(1024)S(1)}, u32[]{:S(2)}) copy-start(f32[1024]{0:T(1024)S(1)} %fusion.128) | copy-start | bytes 12292
  150.5 23.5 %copy-start.36 = (bf16[1024,512]{1,0:T(8,128)(2,1)S(1)}, bf16[1024,512]{1,0:T(8,128)(2,1)}, u32[]{:S(2)}) copy-start(bf16[1024,512]{1,0:T(8,128)(2,1)} %param.29) | copy-start | bytes 3145732
  150.5 23.5 %copy-start.156 = (bf16[2048,512]{1,0:T(8,128)(2,1)S(1)}, bf16[2048,512]{1,0:T(8,128)(2,1)}, u32[]{:S(2)}) copy-start(bf16[2048,512]{1,0:T(8,128)(2,1)} %param.28) | copy-start | bytes 6291460
  185.5 8.8 %copy-start.13 = (f32[1024,512]{1,0:T(8,128)}, f32[1024,512]{1,0:T(8,128)S(1)}, u32[]{:S(2)}) copy-start(f32[1024,512]{1,0:T(8,128)S(1)} %get-tuple-element.84) | copy-start | bytes 6291460
  187.0 177.0 %reduce-scatter.5.cloned.1.call-start = ((), (), s32[]{:S(2)}) async-start(), calls=%async_computation.5 | async-start | bytes 3145728 | tf_op jit(solution)/shard_map/reduce_scatter | solution.py:237
  227.4 7.2 %copy-start.40 = (f32[8,4,8,32]{3,2,1,0:T(8,128)S(1)}, f32[8,4,8,32]{3,2,1,0:T(8,128)}, u32[]{:S(2)}) copy-start(f32[8,4,8,32]{3,2,1,0:T(8,128)} %copy-done.39) | copy-start | bytes 98308
  275.5 7.2 %copy-start.9 = (bf16[8,8,32,4,64]{4,1,3,2,0:T(8,128)(2,1)S(1)}, bf16[8,8,32,4,64]{4,1,3,2,0:T(8,128)(2,1)}, u32[]{:S(2)}) copy-start(bf16[8,8,32,4,64]{4,1,3,2,0:T(8,128)(2,1)} %copy-done.8) | copy-start | bytes 3145732
  308.1 7.0 %copy-start.38 = (f32[8,8,8]{2,1,0:T(8,128)S(1)}, f32[8,8,8]{2,1,0:T(8,128)}, u32[]{:S(2)}) copy-start(f32[8,8,8]{2,1,0:T(8,128)} %copy-done.37) | copy-start | bytes 6148
  308.1 7.0 %copy-start.85 = (f32[8,8]{1,0:T(8,128)S(1)}, f32[8,8]{1,0:T(8,128)}, u32[]{:S(2)}) copy-start(f32[8,8]{1,0:T(8,128)} %copy-done.84) | copy-start | bytes 772
  308.1 7.0 %copy-start.100 = (f32[8,8]{1,0:T(8,128)S(1)}, f32[8,8]{1,0:T(8,128)}, u32[]{:S(2)}) copy-start(f32[8,8]{1,0:T(8,128)} %copy-done.99) | copy-start | bytes 772
  308.1 7.4 %copy-start.126 = (f32[8,8]{1,0:T(8,128)S(1)}, f32[8,8]{1,0:T(8,128)}, u32[]{:S(2)}) copy-start(f32[8,8]{1,0:T(8,128)} %copy-done.125) | copy-start | bytes 772
  308.1 7.4 %copy-start.83 = (f32[8,8]{1,0:T(8,128)S(1)}, f32[8,8]{1,0:T(8,128)}, u32[]{:S(2)}) copy-start(f32[8,8]{1,0:T(8,128)} %copy-done.82) | copy-start | bytes 772
  308.1 7.7 %copy-start.140 = (f32[8,8]{1,0:T(8,128)S(1)}, f32[8,8]{1,0:T(8,128)}, u32[]{:S(2)}) copy-start(f32[8,8]{1,0:T(8,128)} %copy-done.139) | copy-start | bytes 772
  308.2 7.7 %copy-start.23 = (f32[8,8,8]{2,1,0:T(8,128)S(1)}, f32[8,8,8]{2,1,0:T(8,128)}, u32[]{:S(2)}) copy-start(f32[8,8,8]{2,1,0:T(8,128)} %copy-done.22) | copy-start | bytes 6148
  308.2 7.7 %copy-start.47 = (f32[8,8]{1,0:T(8,128)S(1)}, f32[8,8]{1,0:T(8,128)}, u32[]{:S(2)}) copy-start(f32[8,8]{1,0:T(8,128)} %copy-done.46) | copy-start | bytes 772
  308.2 7.7 %copy-start.61 = (f32[8,8]{1,0:T(8,128)S(1)}, f32[8,8]{1,0:T(8,128)}, u32[]{:S(2)}) copy-start(f32[8,8]{1,0:T(8,128)} %copy-done.60) | copy-start | bytes 772
  308.2 7.7 %copy-start.91 = (f32[8,8]{1,0:T(8,128)S(1)}, f32[8,8]{1,0:T(8,128)}, u32[]{:S(2)}) copy-start(f32[8,8]{1,0:T(8,128)} %copy-done.90) | copy-start | bytes 772
  308.2 7.7 %copy-start.106 = (f32[8,8]{1,0:T(8,128)S(1)}, f32[8,8]{1,0:T(8,128)}, u32[]{:S(2)}) copy-start(f32[8,8]{1,0:T(8,128)} %copy-done.105) | copy-start | bytes 772
  308.2 8.0 %copy-start.124 = (f32[8,8]{1,0:T(8,128)S(1)}, f32[8,8]{1,0:T(8,128)}, u32[]{:S(2)}) copy-start(f32[8,8]{1,0:T(8,128)} %copy-done.123) | copy-start | bytes 772
  308.2 8.0 %copy-start.75 = (f32[8,8]{1,0:T(8,128)S(1)}, f32[8,8]{1,0:T(8,128)}, u32[]{:S(2)}) copy-start(f32[8,8]{1,0:T(8,128)} %copy-done.74) | copy-start | bytes 772
  308.2 8.3 %copy-start.138 = (f32[8,8]{1,0:T(8,128)S(1)}, f32[8,8]{1,0:T(8,128)}, u32[]{:S(2)}) copy-start(f32[8,8]{1,0:T(8,128)} %copy-done.137) | copy-start | bytes 772
  308.2 8.3 %copy-start.98 = (f32[8,8]{1,0:T(8,128)S(1)}, f32[8,8]{1,0:T(8,128)}, u32[]{:S(2)}) copy-start(f32[8,8]{1,0:T(8,128)} %copy-done.97) | copy-start | bytes 772
  308.2 8.6 %copy-start.122 = (f32[8,8]{1,0:T(8,128)S(1)}, f32[8,8]{1,0:T(8,128)}, u32[]{:S(2)}) copy-start(f32[8,8]{1,0:T(8,128)} %copy-done.121) | copy-start | bytes 772
  308.3 8.7 %copy-start.81 = (f32[8,8]{1,0:T(8,128)S(1)}, f32[8,8]{1,0:T(8,128)}, u32[]{:S(2)}) copy-start(f32[8,8]{1,0:T(8,128)} %copy-done.80) | copy-start | bytes 772
  308.3 8.9 %copy-start.136 = (f32[8,8]{1,0:T(8,128)S(1)}, f32[8,8]{1,0:T(8,128)}, u32[]{:S(2)}) copy-start(f32[8,8]{1,0:T(8,128)} %copy-done.135) | copy-start | bytes 772
  308.3 9.0 %copy-start.21 = (f32[8,8,8]{2,1,0:T(8,128)S(1)}, f32[8,8,8]{2,1,0:T(8,128)}, u32[]{:S(2)}) copy-start(f32[8,8,8]{2,1,0:T(8,128)} %copy-done.20) | copy-start | bytes 6148
  308.3 9.0 %copy-start.45 = (f32[8,8]{1,0:T(8,128)S(1)}, f32[8,8]{1,0:T(8,128)}, u32[]{:S(2)}) copy-start(f32[8,8]{1,0:T(8,128)} %copy-done.44) | copy-start | bytes 772
  308.3 9.0 %copy-start.59 = (f32[8,8]{1,0:T(8,128)S(1)}, f32[8,8]{1,0:T(8,128)}, u32[]{:S(2)}) copy-start(f32[8,8]{1,0:T(8,128)} %copy-done.58) | copy-start | bytes 772
  308.3 9.0 %copy-start.89 = (f32[8,8]{1,0:T(8,128)S(1)}, f32[8,8]{1,0:T(8,128)}, u32[]{:S(2)}) copy-start(f32[8,8]{1,0:T(8,128)} %copy-done.88) | copy-start | bytes 772
  308.3 9.0 %copy-start.104 = (f32[8,8]{1,0:T(8,128)S(1)}, f32[8,8]{1,0:T(8,128)}, u32[]{:S(2)}) copy-start(f32[8,8]{1,0:T(8,128)} %copy-done.103) | copy-start | bytes 772
  308.3 9.3 %copy-start.120 = (f32[8,8]{1,0:T(8,128)S(1)}, f32[8,8]{1,0:T(8,128)}, u32[]{:S(2)}) copy-start(f32[8,8]{1,0:T(8,128)} %copy-done.119) | copy-start | bytes 772
  308.3 9.3 %copy-start.73 = (f32[8,8]{1,0:T(8,128)S(1)}, f32[8,8]{1,0:T(8,128)}, u32[]{:S(2)}) copy-start(f32[8,8]{1,0:T(8,128)} %copy-done.72) | copy-start | bytes 772
  308.4 9.6 %copy-start.134 = (f32[8,8]{1,0:T(8,128)S(1)}, f32[8,8]{1,0:T(8,128)}, u32[]{:S(2)}) copy-start(f32[8,8]{1,0:T(8,128)} %copy-done.133) | copy-start | bytes 772
  308.4 9.6 %copy-start.96 = (f32[8,8]{1,0:T(8,128)S(1)}, f32[8,8]{1,0:T(8,128)}, u32[]{:S(2)}) copy-start(f32[8,8]{1,0:T(8,128)} %copy-done.95) | copy-start | bytes 772
  314.3 12.5 %copy-start.24 = (bf16[2048,256]{1,0:T(8,128)(2,1)}, bf16[2048,256]{1,0:T(8,128)(2,1)S(1)}, u32[]{:S(2)}) copy-start(bf16[2048,256]{1,0:T(8,128)(2,1)S(1)} %reshape.619) | copy-start | bytes 3145732
  316.6 9.5 %copy-start.64 = (bf16[512,256]{1,0:T(8,128)(2,1)S(1)}, bf16[512,256]{1,0:T(8,128)(2,1)}, u32[]{:S(2)}) copy-start(bf16[512,256]{1,0:T(8,128)(2,1)} %param.20) | copy-start | bytes 786436
  330.9 136.2 %all-reduce.8.cloned.1.call-start = ((), (), s32[]{:S(2)}) async-start(), calls=%async_computation.7 | async-start | bytes 4194304 | tf_op jit(solution)/shard_map/psum | solution.py:248
  340.5 325.5 %all-reduce.6.cloned.1.call-start = ((), (), s32[]{:S(2)}) async-start(), calls=%async_computation.6 | async-start | bytes 18874368 | tf_op jit(solution)/shard_map/psum | solution.py:253
  346.0 7.4 %copy-start.51 = (bf16[512,512]{1,0:T(8,128)(2,1)S(1)}, bf16[512,512]{1,0:T(8,128)(2,1)}, u32[]{:S(2)}) copy-start(bf16[512,512]{1,0:T(8,128)(2,1)} %param.23) | copy-start | bytes 1572868
  352.3 12.3 %copy-start.69 = (f32[1024]{0:T(1024)S(1)}, f32[1024]{0:T(1024)}, u32[]{:S(2)}) copy-start(f32[1024]{0:T(1024)} %copy-done.68) | copy-start | bytes 12292
  352.3 12.3 %copy-start.145 = (f32[512]{0:T(512)S(1)}, f32[512]{0:T(512)}, u32[]{:S(2)}) copy-start(f32[512]{0:T(512)} %param.17) | copy-start | bytes 6148
  353.4 11.2 %dynamic-slice-start = ((f32[2048]{0:T(1024)}, s32[]{:T(128)}), f32[1024]{0:T(1024)S(1)}, s32[]{:S(2)}) async-start(f32[2048]{0:T(1024)} %copy-done.146, s32[]{:T(128)} %select_n.18), calls=%async_computation.8 | async-start | bytes 8704 | tf_op jit(solution)/shard_map/dynamic_slice | solution.py:245
  665.9 9.9 %copy-start.34 = (f32[512,2048]{1,0:T(8,128)S(1)}, f32[512,2048]{1,0:T(8,128)}, u32[]{:S(2)}) copy-start(f32[512,2048]{1,0:T(8,128)} %get-tuple-element.128) | copy-start | bytes 12582916
  (103 other events, 293.9 us)
Sparse Core Ops, SparseCore 0:
  13.4 35.8 all-gather.2
  115.2 31.8 reduce-scatter.2
  187.1 33.1 all-gather.4
  331.0 33.0 reduce-scatter.4
  368.4 98.5 all-reduce.7
  474.6 191.2 all-reduce.5
where the time goes:
time: 695 us; the launch traced here: 689 us
  waiting for transfers between devices  352 us (51%)
  matrix products  137 us (20%)
  local copies, waits for them, and re-layouts  75.9 us (11%)
  other arithmetic  58.7 us (8%)
  blocking collectives  47.5 us (7%)
  between operations  17.1 us (2%)
    psum x1, waiting for transfers between devices, on_device(): lax.psum((grad_gain_one, grad_bias_one, grad_first * sort_share, grad_sec...  199 us
    psum x1, waiting for transfers between devices, on_device(): lax.psum((grad_w_query, grad_w_key, grad_w_value, grad_w_out), 'dp')  55.9 us
    psum x1, blocking collectives, on_device(): lax.psum((grad_gain_one, grad_bias_one, grad_first * sort_share, grad_sec...  40.3 us
    all_gather x1, waiting for transfers between devices, on_device(): normed_here = lax.all_gather(normed, 'head', axis=0, tiled=True)  33.3 us
    reduce_scatter x1, waiting for transfers between devices, on_device(): lax.psum_scatter(jnp.dot(mixed_rows, w_out, preferred_element_type=jnp.fl...  31.9 us
    unnamed x327, local copies, waits for them, and re-layouts  31.9 us
    dot_general x1, matrix products, on_device(): up_value = jnp.dot(normed_two, w_up, preferred_element_type=jnp.float32)  23.5 us
    all_gather x1, waiting for transfers between devices, on_device(): lax.all_gather(grad_attention, 'head', axis=0, tiled=True)  21.4 us
  transfers between devices with their start and end apart: 6, of which 6 were waited for; matrix products, arithmetic and copies ran while one was open for 6% of the time, Pallas kernels for 0%

commit v1 on v0

--- a/solution.py
+++ b/solution.py
@@ -8,6 +8,28 @@
 ITERS = 8
 LMAX = 256
 precise = lax.Precision.HIGHEST
+
+
+def joined_along(pieces, dim):
+    shape = list(pieces.shape[1:])
+    shape[dim] *= pieces.shape[0]
+    return jnp.moveaxis(pieces, 0, dim).reshape(shape)
+
+
+def grow_blocks(shard, axis):
+    count = lax.axis_size(axis)
+    blocks = shard[None]
+    for level in range(count.bit_length() - 1):
+        distance = 1 << level
+        theirs = lax.ppermute(blocks, axis, [(i, i ^ distance) for i in range(count)])
+        both = jnp.stack([blocks, theirs])
+        upper = lax.axis_index(axis) >> level & 1
+        blocks = jnp.where(upper == 0, both, both[::-1]).reshape(-1, *shard.shape)
+    return blocks
+
+
+def collect(shard, axis, dim):
+    return joined_along(grow_blocks(shard, axis), dim)
 
 
 def smooth_gate(values):
@@ -212,7 +234,7 @@
     )
     grad_middle = cotangent.astype(jnp.float32) + grad_middle_norm
     grad_attention = grad_middle.astype(jnp.bfloat16)
-    grad_attention_here = lax.all_gather(grad_attention, "head", axis=0, tiled=True)
+    grad_attention_here = collect(grad_attention, "head", 0)
     grad_w_out = outer_product(mixed_rows, grad_attention_here)
     grad_mixed = jnp.dot(
         grad_attention_here, out_rows.T, preferred_element_type=jnp.float32

time: 695 us -> 689 us (level)
  waiting for transfers between devices: 352 us -> 344 us
    all_gather x1 -> x0, waiting for transfers between devices: 21.4 us -> none  [on_device(): lax.all_gather(grad_attention, 'head', axis=0, tiled=True)]
    ppermute x0 -> x1, waiting for transfers between devices: none -> 14.8 us  [grow_blocks(): lax.ppermute(blocks, axis, [(i, i ^ distance) for i in range(count)])]
where the time goes in v1:
time: 689 us; the launch traced here: 683 us
  waiting for transfers between devices  344 us (50%)
  matrix products  135 us (20%)
  local copies, waits for them, and re-layouts  80.8 us (12%)
  other arithmetic  58.6 us (9%)
  blocking collectives  47.6 us (7%)
  between operations  16.7 us (2%)
    psum x1, waiting for transfers between devices, on_device(): lax.psum((grad_gain_one, grad_bias_one, grad_first * sort_share, grad_sec...  199 us
    psum x1, waiting for transfers between devices, on_device(): lax.psum((grad_w_query, grad_w_key, grad_w_value, grad_w_out), 'dp')  54.9 us
    psum x1, blocking collectives, on_device(): lax.psum((grad_gain_one, grad_bias_one, grad_first * sort_share, grad_sec...  40.3 us
    unnamed x327, local copies, waits for them, and re-layouts  33.9 us
    all_gather x1, waiting for transfers between devices, on_device(): normed_here = lax.all_gather(normed, 'head', axis=0, tiled=True)  33.3 us
    reduce_scatter x1, waiting for transfers between devices, on_device(): lax.psum_scatter(jnp.dot(mixed_rows, w_out, preferred_element_type=jnp.fl...  31.9 us
    dot_general x1, matrix products, on_device(): up_value = jnp.dot(normed_two, w_up, preferred_element_type=jnp.float32)  22 us
    dot_general x6, matrix products, outer_product(): lax.dot_general(left, right, (((0,), (0,)), ((), ())), preferred_element_...  17.1 us
  transfers between devices with their start and end apart: 6, of which 6 were waited for; matrix products, arithmetic and copies ran while one was open for 6% of the time, Pallas kernels for 0%

profile of v1, /device:TPU:0, one launch (start us, length us, event | category | flops | bytes accessed | tf_op | source)
XLA Modules:
  0.0 682.6 jit_solution(13769608445741328147)
XLA Ops:
  10.6 2.7 fusion.43
  16.0 33.3 %all-gather.2.cloned.1.call-done = bf16[2048,512]{1,0:T(8,128)(2,1)} async-done(((bf16[1024,512]{1,0:T(8,128)(2,1)}), bf16[2048,512]{1,0:T(8,128)(2,1)}) %all-gather.2.cloned.1.call-update) | async-done | bytes 2097168 | tf_op jit(solution)/shard_map/all_gather | solution.py:205
  49.3 2.9 fusion.17
  67.7 2.7 convolution_convert_fusion.2
  70.4 4.9 reshape.616
  75.3 3.3 convolution_convert_fusion.3
  78.6 4.4 reshape.615
  83.0 2.3 convolution_convert_fusion.4
  85.3 1.8 reshape.614
  87.1 4.9 copy_multiply_fusion.1
  92.0 1.9 convolution_convert_fusion.5
  93.9 1.9 convolution_convert_fusion.6
  95.8 1.8 pad_maximum_fusion
  97.7 2.5 fusion.34
  100.2 2.4 exponential_reduce_fusion
  102.7 2.5 fusion.47
  105.2 2.4 copy.60
  107.6 4.4 convert_element_type.200
  112.0 3.3 convolution_convert_fusion
  115.4 31.9 %reduce-scatter.3.cloned.1.call-done = bf16[1024,512]{1,0:T(8,128)(2,1)} async-done(((bf16[2048,512]{1,0:T(8,128)(2,1)}), bf16[1024,512]{1,0:T(8,128)(2,1)}) %reduce-scatter.3.cloned.1.call-update) | async-done | bytes 1048592 | tf_op jit(solution)/shard_map/reduce_scatter | solution.py:211
  149.0 1.7 multiply_reduce_fusion.3
  150.9 22.0 %multiply_convert_fusion = (bf16[1024,2048]{1,0:T(8,128)(2,1)S(1)}, f32[1024,2048]{1,0:T(8,128)S(1)}, f32[1024,2048]{1,0:T(8,128)}) fusion(bf16[512,2048]{1,0:T(8,128)(2,1)S(1)} %copy-done, bf16[1024,512]{1,0:T(8,128)(2,1)S(1)} %copy-done.29, bf16[1024,512]{1,0:T(8,128)(2,1)S(1)} %copy-done.2, f32[512]{0:T(512)S(1)} %copy-done.157, f32[512]{0:T(512)S(1)} %copy-done.152, ...), kind=kOutput, calls=%fused_computation.12 | convolution fusion | flops 2287992832 | bytes 25178112 | tf_op jit(solution)/shard_map/dot_general | solution.py:220
  172.9 8.4 %fusion.5 = bf16[1024,2048]{1,0:T(8,128)(2,1)S(1)} fusion(f32[1024,2048]{1,0:T(8,128)S(1)} %get-tuple-element.86, f32[1024,2048]{1,0:T(8,128)} %get-tuple-element.110, bf16[1024,512]{1,0:T(8,128)(2,1)S(1)} %copy-done.28, bf16[2048,512]{1,0:T(8,128)(2,1)S(1)} %copy-done.156), kind=kOutput, calls=%fused_computation.8 | convolution fusion | flops 2181038080 | bytes 24117248 | tf_op jit(solution)/shard_map/dot_general | solution.py:226
  181.3 3.3 multiply_reduce_fusion.1
  186.9 4.4 fusion.167
  192.0 4.6 fusion.143
  196.6 14.8 %collective-permute-done = bf16[1,1024,512]{2,1,0:T(8,128)(2,1)S(1)} collective-permute-done((bf16[1,1024,512]{2,1,0:T(8,128)(2,1)S(1)}, bf16[1,1024,512]{2,1,0:T(8,128)(2,1)S(1)}, u32[]{:S(2)}, u32[]{:S(2)}) %collective-permute-start) | collective-permute-done | bytes 1048608 | tf_op jit(solution)/shard_map/ppermute | solution.py:24
  212.4 1.7 convolution_convert_fusion.1
  214.1 4.4 reshape.617
  218.6 3.0 copy_multiply_fusion
  221.6 7.2 %multiply_reduce_fusion = (f32[8,8,4,32]{3,2,1,0:T(4,128)S(1)}, f32[8,8,4,32,64]{4,3,2,1,0:T(8,128)S(1)}) fusion(f32[8,8,4,32,64]{4,3,2,1,0:T(8,128)S(1)} %copy-done.4, f32[8,8,4,32]{3,2,1,0:T(4,128)} %bitcast.112, pred[8,8,32,64]{3,2,1,0:T(8,128)(4,1)S(1)} %broadcast_or_fusion, bf16[8,8,64,4,64]{4,1,3,2,0:T(8,128)(2,1)} %copy-done.38, ...), kind=kOutput, calls=%fused_computation.47 | convolution fusion | flops 69722112 | bytes 7536640 | tf_op jit(solution)/shard_map/cibhd,cikhd->cihbk/dot_general | solution.py:103
  228.8 6.0 convolution_bitcast_fusion
  234.8 2.5 multiply_convert_fusion.2
  240.8 3.1 copy-done.7
  243.9 6.4 fusion.65
  250.3 7.6 %fusion.24 = f32[8,8,32,4,64]{4,1,3,2,0:T(8,128)} fusion(f32[8,8,32,4,64]{4,2,3,1,0:T(8,128)S(1)} %slice.17, f32[8,8,8]{2,1,0:T(8,128)S(1)} %get-tuple-element.88, f32[8,8]{1,0:T(8,128)S(1)} %log_add_fusion.1, f32[8,8]{1,0:T(8,128)S(1)} %log_add_fusion.2), kind=kOutput, calls=%fused_computation.42 | convolution fusion | flops 50332672 | bytes 4196864 | tf_op jit(solution)/shard_map/cij,cithd->cjthd/dot_general | solution.py:127
  257.9 2.4 copy.65
  260.3 3.5 reshape.618
  263.8 2.8 fusion.161
  266.6 3.0 slice.19
  269.6 7.2 %fusion.22 = f32[8,8,32,4,64]{4,1,3,2,0:T(8,128)} fusion(f32[8,8,32,4,64]{4,2,3,1,0:T(8,128)S(1)} %slice.19, f32[8,8,8]{2,1,0:T(8,128)S(1)} %get-tuple-element.88, f32[8,8]{1,0:T(8,128)S(1)} %log_add_fusion.1, f32[8,8]{1,0:T(8,128)S(1)} %log_add_fusion.2), kind=kOutput, calls=%fused_computation.40 | convolution fusion | flops 50332672 | bytes 4196864 | tf_op jit(solution)/shard_map/cij,cithd->cjthd/dot_general | solution.py:130
  276.8 5.5 fusion.75
  282.3 7.3 %psum.91 = f32[8,8,8]{2,1,0:T(8,128)S(1)} all-reduce(f32[8,8,8]{2,1,0:T(8,128)S(1)} %fusion.75), channel_id=1, replica_groups=mesh['dp'=16,'head'=2] {'head'}, use_global_device_ids=true, to_apply=%region_44.45 | all-reduce | flops 512 | bytes 4096 | tf_op jit(solution)/shard_map/psum | solution.py:245
  289.6 12.7 %fusion.14 = (bf16[8,8,32,4,64]{4,2,3,1,0:T(8,128)(2,1)S(1)}, bf16[8,8,32,4,64]{4,2,3,1,0:T(8,128)(2,1)}) fusion(f32[8,8,64,4,64]{4,2,3,1,0:T(8,128)} %convolution_bitcast_fusion, f32[8,8,32,4,64]{4,1,3,2,0:T(8,128)} %fusion.22, f32[8,8,32]{2,1,0:T(8,128)S(1)} %get-tuple-element.101, f32[8,8,32,4,64]{4,1,3,2,0:T(8,128)} %fusion.24, ...), kind=kLoop, calls=%fused_computation.28 | loop fusion | flops 3145728 | bytes 10493952 | tf_op jit(solution)/shard_map/convert_element_type | solution.py:137
  302.6 2.5 copy.75
  305.1 3.5 reshape.620
  312.5 4.1 copy.70
  316.6 3.7 reshape.619
  323.0 2.1 add_convert_fusion
  326.6 3.4 fusion.166
  336.1 2.9 fusion.63
  340.2 6.3 add_convert_fusion.2
  348.2 9.9 %reduce-scatter.5.cloned.1.call-done = bf16[1024,512]{1,0:T(8,128)(2,1)} async-done(((bf16[2048,512]{1,0:T(8,128)(2,1)}), bf16[1024,512]{1,0:T(8,128)(2,1)}) %reduce-scatter.5.cloned.1.call-update) | async-done | bytes 1048592 | tf_op jit(solution)/shard_map/reduce_scatter | solution.py:259
  363.0 40.3 %all-reduce = (f32[512]{0:T(512)}, f32[512]{0:T(512)}, f32[512,8]{0,1:T(8,128)}, f32[512]{0:T(512)}, f32[512]{0:T(512)}) all-reduce(f32[512]{0:T(512)S(1)} %get-tuple-element.16, f32[512]{0:T(512)S(1)} %get-tuple-element.19, f32[512,8]{0,1:T(8,128)S(1)} %fusion.80, ...), channel_id=1, replica_groups=mesh['dp'=16,'head'=2] {'dp','head'}, use_global_device_ids=true, to_apply=%region_96.97 | all-reduce | flops 6144 | bytes 49152 | tf_op jit(solution)/shard_map/psum | solution.py:275
  403.3 3.3 add_convert_fusion.1
  406.6 54.9 %all-reduce.8.cloned.1.call-done = (f32[512,256]{1,0:T(8,128)}, f32[512,256]{1,0:T(8,128)}, f32[512,256]{1,0:T(8,128)}, f32[256,512]{1,0:T(8,128)}) async-done(((f32[512,256]{1,0:T(8,128)}, f32[512,256]{1,0:T(8,128)}, f32[512,256]{1,0:T(8,128)}, f32[256,512]{1,0:T(8,128)}), (f32[512,256]{1,0:T(8,128)}, f32[512,256]{1,0:T(8,128)}, f32[512,256]{1,0:T(8,128)}, ...) | async-done | bytes 2097168 | tf_op jit(solution)/shard_map/psum | solution.py:270
  461.4 198.8 %all-reduce.6.cloned.1.call-done = (f32[512,512]{1,0:T(8,128)}, f32[512,2048]{1,0:T(8,128)}, f32[2048,512]{1,0:T(8,128)}) async-done(((f32[512,512]{1,0:T(8,128)}, f32[512,2048]{1,0:T(8,128)}, f32[2048,512]{1,0:T(8,128)}), (f32[512,512]{1,0:T(8,128)}, f32[512,2048]{1,0:T(8,128)}, f32[2048,512]{1,0:T(8,128)})) %all-reduce.6.cloned.1.call-update) | async-done | bytes 9437200 | tf_op jit(solution)/shard_map/psum | solution.py:275
  660.3 2.0 copy.155
  662.3 1.9 copy.156
  664.2 1.9 copy.157
  666.0 1.9 copy.158
  667.9 2.3 copy.159
  670.2 2.1 copy.160
  673.9 2.0 copy.161
  (486 shorter events, 52.7 us)
Async XLA Ops:
  7.2 143.6 %copy-start = (bf16[512,2048]{1,0:T(8,128)(2,1)S(1)}, bf16[512,2048]{1,0:T(8,128)(2,1)}, u32[]{:S(2)}) copy-start(bf16[512,2048]{1,0:T(8,128)(2,1)} %param.27) | copy-start | bytes 6291460
  7.2 45.0 %copy-start.53 = (bf16[512,512]{1,0:T(8,128)(2,1)S(1)}, bf16[512,512]{1,0:T(8,128)(2,1)}, u32[]{:S(2)}) copy-start(bf16[512,512]{1,0:T(8,128)(2,1)} %param.23) | copy-start | bytes 1572868
  7.2 42.1 %all-gather.2.cloned.1.call-start = ((), (), s32[]{:S(2)}) async-start(), calls=%async_computation.2 | async-start | bytes 3145728 | tf_op jit(solution)/shard_map/all_gather | solution.py:205
  8.9 44.3 %copy-start.150 = (bf16[512,8]{0,1:T(8,128)(2,1)S(1)}, bf16[512,8]{0,1:T(8,128)(2,1)}, u32[]{:S(2)}) copy-start(bf16[512,8]{0,1:T(8,128)(2,1)} %param.24) | copy-start | bytes 24580
  8.9 40.4 %copy-start.71 = (f32[1024]{0:T(1024)}, f32[1024]{0:T(1024)S(1)}, u32[]{:S(2)}) copy-start(f32[1024]{0:T(1024)S(1)} %broadcast_multiply_fusion.1) | copy-start | bytes 12292
  10.6 38.7 %copy-start.114 = (f32[1024]{0:T(1024)}, f32[1024]{0:T(1024)S(1)}, u32[]{:S(2)}) copy-start(f32[1024]{0:T(1024)S(1)} %fusion.45) | copy-start | bytes 12292
  10.6 38.7 %copy-start.110 = (f32[1024]{0:T(1024)}, f32[1024]{0:T(1024)S(1)}, u32[]{:S(2)}) copy-start(f32[1024]{0:T(1024)S(1)} %fusion.127) | copy-start | bytes 12292
  13.3 134.1 %reduce-scatter.3.cloned.1.call-start = ((), (), s32[]{:S(2)}) async-start(), calls=%async_computation.3 | async-start | bytes 3145728 | tf_op jit(solution)/shard_map/reduce_scatter | solution.py:211
  13.5 276.1 %copy-start.51 = (f32[8,8,32]{2,1,0:T(8,128)}, f32[8,8,32]{2,1,0:T(8,128)S(1)}, u32[]{:S(2)}) copy-start(f32[8,8,32]{2,1,0:T(8,128)S(1)} %get-tuple-element.101) | copy-start | bytes 24580
  49.3 18.4 %copy-start.5 = (bf16[2048,512]{1,0:T(8,128)(2,1)S(1)}, bf16[2048,512]{1,0:T(8,128)(2,1)}, u32[]{:S(2)}) copy-start(bf16[2048,512]{1,0:T(8,128)(2,1)} %all-gather.2.cloned.1.call-done) | copy-start | bytes 6291460
  52.6 22.6 %copy-start.55 = (f32[8,8,512]{2,1,0:T(8,128)}, f32[8,8,512]{2,1,0:T(8,128)S(1)}, u32[]{:S(2)}) copy-start(f32[8,8,512]{2,1,0:T(8,128)S(1)} %get-tuple-element.105) | copy-start | bytes 393220
  53.1 22.2 %copy-start.57 = (f32[8,8,512]{2,1,0:T(8,128)}, f32[8,8,512]{2,1,0:T(8,128)S(1)}, u32[]{:S(2)}) copy-start(f32[8,8,512]{2,1,0:T(8,128)S(1)} %fusion.85) | copy-start | bytes 393220
  54.9 8.0 %copy-start.45 = (f32[8,8]{1,0:T(8,128)}, f32[8,8]{1,0:T(8,128)S(1)}, u32[]{:S(2)}) copy-start(f32[8,8]{1,0:T(8,128)S(1)} %log_add_fusion.16) | copy-start | bytes 772
  55.6 10.2 %copy-start.59 = (f32[8,8]{1,0:T(8,128)}, f32[8,8]{1,0:T(8,128)S(1)}, u32[]{:S(2)}) copy-start(f32[8,8]{1,0:T(8,128)S(1)} %log_add_fusion.15) | copy-start | bytes 772
  58.0 17.2 %copy-start.22 = (f32[8,8,8]{2,1,0:T(8,128)}, f32[8,8,8]{2,1,0:T(8,128)S(1)}, u32[]{:S(2)}) copy-start(f32[8,8,8]{2,1,0:T(8,128)S(1)} %get-tuple-element.94) | copy-start | bytes 6148
  61.0 14.3 %copy-start.24 = (f32[8,8,8]{2,1,0:T(8,128)}, f32[8,8,8]{2,1,0:T(8,128)S(1)}, u32[]{:S(2)}) copy-start(f32[8,8,8]{2,1,0:T(8,128)S(1)} %get-tuple-element.92) | copy-start | bytes 6148
  61.6 13.7 %copy-start.49 = (f32[8,8]{1,0:T(8,128)}, f32[8,8]{1,0:T(8,128)S(1)}, u32[]{:S(2)}) copy-start(f32[8,8]{1,0:T(8,128)S(1)} %log_add_fusion.8) | copy-start | bytes 772
  63.6 11.7 %copy-start.39 = (f32[8,8,8]{2,1,0:T(8,128)}, f32[8,8,8]{2,1,0:T(8,128)S(1)}, u32[]{:S(2)}) copy-start(f32[8,8,8]{2,1,0:T(8,128)S(1)} %get-tuple-element.90) | copy-start | bytes 6148
  67.7 7.6 %copy-start.65 = (bf16[512,256]{1,0:T(8,128)(2,1)S(1)}, bf16[512,256]{1,0:T(8,128)(2,1)}, u32[]{:S(2)}) copy-start(bf16[512,256]{1,0:T(8,128)(2,1)} %param.19) | copy-start | bytes 786436
  107.6 39.8 %copy-start.2 = (bf16[1024,512]{1,0:T(8,128)(2,1)S(1)}, bf16[1024,512]{1,0:T(8,128)(2,1)}, u32[]{:S(2)}) copy-start(bf16[1024,512]{1,0:T(8,128)(2,1)} %param.15) | copy-start | bytes 3145732
  112.0 38.8 %copy-start.152 = (f32[512]{0:T(512)S(1)}, f32[512]{0:T(512)}, u32[]{:S(2)}) copy-start(f32[512]{0:T(512)} %param.25) | copy-start | bytes 6148
  112.0 38.8 %copy-start.157 = (f32[512]{0:T(512)S(1)}, f32[512]{0:T(512)}, u32[]{:S(2)}) copy-start(f32[512]{0:T(512)} %param.26) | copy-start | bytes 6148
  115.4 242.8 %reduce-scatter.5.cloned.1.call-start = ((), (), s32[]{:S(2)}) async-start(), calls=%async_computation.4 | async-start | bytes 3145728 | tf_op jit(solution)/shard_map/reduce_scatter | solution.py:259
  150.8 22.1 %copy-start.28 = (bf16[1024,512]{1,0:T(8,128)(2,1)S(1)}, bf16[1024,512]{1,0:T(8,128)(2,1)}, u32[]{:S(2)}) copy-start(bf16[1024,512]{1,0:T(8,128)(2,1)} %param.29) | copy-start | bytes 3145732
  150.8 22.0 %copy-start.156 = (bf16[2048,512]{1,0:T(8,128)(2,1)S(1)}, bf16[2048,512]{1,0:T(8,128)(2,1)}, u32[]{:S(2)}) copy-start(bf16[2048,512]{1,0:T(8,128)(2,1)} %param.28) | copy-start | bytes 6291460
  172.9 14.0 %copy-start.159 = (bf16[1024,2048]{1,0:T(8,128)(2,1)}, bf16[1024,2048]{1,0:T(8,128)(2,1)S(1)}, u32[]{:S(2)}) copy-start(bf16[1024,2048]{1,0:T(8,128)(2,1)S(1)} %get-tuple-element.85) | copy-start | bytes 12582916
  186.5 25.0 %collective-permute-start = (bf16[1,1024,512]{2,1,0:T(8,128)(2,1)S(1)}, bf16[1,1024,512]{2,1,0:T(8,128)(2,1)S(1)}, u32[]{:S(2)}, u32[]{:S(2)}) collective-permute-start(bf16[1,1024,512]{2,1,0:T(8,128)(2,1)S(1)} %fusion.209), channel_id=1, source_target_pairs={{0,1},{1,0},{2,3},{3,2},{4,5},{5,4},{6,7},{7,6},{8,9},{9,8},{10,11... | collective-permute-start | bytes 3145736 | tf_op jit(solution)/shard_map/ppermute | solution.py:24
  221.6 7.2 %copy-start.42 = (f32[8,4,8,32]{3,2,1,0:T(8,128)S(1)}, f32[8,4,8,32]{3,2,1,0:T(8,128)}, u32[]{:S(2)}) copy-start(f32[8,4,8,32]{3,2,1,0:T(8,128)} %copy-done.41) | copy-start | bytes 98308
  269.6 7.2 %copy-start.11 = (bf16[8,8,32,4,64]{4,1,3,2,0:T(8,128)(2,1)S(1)}, bf16[8,8,32,4,64]{4,1,3,2,0:T(8,128)(2,1)}, u32[]{:S(2)}) copy-start(bf16[8,8,32,4,64]{4,1,3,2,0:T(8,128)(2,1)} %copy-done.10) | copy-start | bytes 3145732
  302.4 7.0 %copy-start.40 = (f32[8,8,8]{2,1,0:T(8,128)S(1)}, f32[8,8,8]{2,1,0:T(8,128)}, u32[]{:S(2)}) copy-start(f32[8,8,8]{2,1,0:T(8,128)} %copy-done.39) | copy-start | bytes 6148
  302.4 7.4 %copy-start.129 = (f32[8,8]{1,0:T(8,128)S(1)}, f32[8,8]{1,0:T(8,128)}, u32[]{:S(2)}) copy-start(f32[8,8]{1,0:T(8,128)} %copy-done.128) | copy-start | bytes 772
  302.4 7.4 %copy-start.86 = (f32[8,8]{1,0:T(8,128)S(1)}, f32[8,8]{1,0:T(8,128)}, u32[]{:S(2)}) copy-start(f32[8,8]{1,0:T(8,128)} %copy-done.85) | copy-start | bytes 772
  302.4 7.7 %copy-start.143 = (f32[8,8]{1,0:T(8,128)S(1)}, f32[8,8]{1,0:T(8,128)}, u32[]{:S(2)}) copy-start(f32[8,8]{1,0:T(8,128)} %copy-done.142) | copy-start | bytes 772
  302.4 7.7 %copy-start.25 = (f32[8,8,8]{2,1,0:T(8,128)S(1)}, f32[8,8,8]{2,1,0:T(8,128)}, u32[]{:S(2)}) copy-start(f32[8,8,8]{2,1,0:T(8,128)} %copy-done.24) | copy-start | bytes 6148
  302.4 7.7 %copy-start.50 = (f32[8,8]{1,0:T(8,128)S(1)}, f32[8,8]{1,0:T(8,128)}, u32[]{:S(2)}) copy-start(f32[8,8]{1,0:T(8,128)} %copy-done.49) | copy-start | bytes 772
  302.4 7.7 %copy-start.64 = (f32[8,8]{1,0:T(8,128)S(1)}, f32[8,8]{1,0:T(8,128)}, u32[]{:S(2)}) copy-start(f32[8,8]{1,0:T(8,128)} %copy-done.63) | copy-start | bytes 772
  302.5 7.7 %copy-start.94 = (f32[8,8]{1,0:T(8,128)S(1)}, f32[8,8]{1,0:T(8,128)}, u32[]{:S(2)}) copy-start(f32[8,8]{1,0:T(8,128)} %copy-done.93) | copy-start | bytes 772
  302.5 7.7 %copy-start.109 = (f32[8,8]{1,0:T(8,128)S(1)}, f32[8,8]{1,0:T(8,128)}, u32[]{:S(2)}) copy-start(f32[8,8]{1,0:T(8,128)} %copy-done.108) | copy-start | bytes 772
  302.5 8.0 %copy-start.127 = (f32[8,8]{1,0:T(8,128)S(1)}, f32[8,8]{1,0:T(8,128)}, u32[]{:S(2)}) copy-start(f32[8,8]{1,0:T(8,128)} %copy-done.126) | copy-start | bytes 772
  302.5 8.0 %copy-start.78 = (f32[8,8]{1,0:T(8,128)S(1)}, f32[8,8]{1,0:T(8,128)}, u32[]{:S(2)}) copy-start(f32[8,8]{1,0:T(8,128)} %copy-done.77) | copy-start | bytes 772
  302.5 8.3 %copy-start.141 = (f32[8,8]{1,0:T(8,128)S(1)}, f32[8,8]{1,0:T(8,128)}, u32[]{:S(2)}) copy-start(f32[8,8]{1,0:T(8,128)} %copy-done.140) | copy-start | bytes 772
  302.5 8.3 %copy-start.101 = (f32[8,8]{1,0:T(8,128)S(1)}, f32[8,8]{1,0:T(8,128)}, u32[]{:S(2)}) copy-start(f32[8,8]{1,0:T(8,128)} %copy-done.100) | copy-start | bytes 772
  302.5 8.6 %copy-start.125 = (f32[8,8]{1,0:T(8,128)S(1)}, f32[8,8]{1,0:T(8,128)}, u32[]{:S(2)}) copy-start(f32[8,8]{1,0:T(8,128)} %copy-done.124) | copy-start | bytes 772
  302.5 8.7 %copy-start.84 = (f32[8,8]{1,0:T(8,128)S(1)}, f32[8,8]{1,0:T(8,128)}, u32[]{:S(2)}) copy-start(f32[8,8]{1,0:T(8,128)} %copy-done.83) | copy-start | bytes 772
  302.5 8.9 %copy-start.139 = (f32[8,8]{1,0:T(8,128)S(1)}, f32[8,8]{1,0:T(8,128)}, u32[]{:S(2)}) copy-start(f32[8,8]{1,0:T(8,128)} %copy-done.138) | copy-start | bytes 772
  302.5 9.0 %copy-start.23 = (f32[8,8,8]{2,1,0:T(8,128)S(1)}, f32[8,8,8]{2,1,0:T(8,128)}, u32[]{:S(2)}) copy-start(f32[8,8,8]{2,1,0:T(8,128)} %copy-done.22) | copy-start | bytes 6148
  302.6 9.0 %copy-start.48 = (f32[8,8]{1,0:T(8,128)S(1)}, f32[8,8]{1,0:T(8,128)}, u32[]{:S(2)}) copy-start(f32[8,8]{1,0:T(8,128)} %copy-done.47) | copy-start | bytes 772
  302.6 9.0 %copy-start.62 = (f32[8,8]{1,0:T(8,128)S(1)}, f32[8,8]{1,0:T(8,128)}, u32[]{:S(2)}) copy-start(f32[8,8]{1,0:T(8,128)} %copy-done.61) | copy-start | bytes 772
  302.6 9.0 %copy-start.92 = (f32[8,8]{1,0:T(8,128)S(1)}, f32[8,8]{1,0:T(8,128)}, u32[]{:S(2)}) copy-start(f32[8,8]{1,0:T(8,128)} %copy-done.91) | copy-start | bytes 772
  302.6 9.0 %copy-start.107 = (f32[8,8]{1,0:T(8,128)S(1)}, f32[8,8]{1,0:T(8,128)}, u32[]{:S(2)}) copy-start(f32[8,8]{1,0:T(8,128)} %copy-done.106) | copy-start | bytes 772
  302.6 9.3 %copy-start.123 = (f32[8,8]{1,0:T(8,128)S(1)}, f32[8,8]{1,0:T(8,128)}, u32[]{:S(2)}) copy-start(f32[8,8]{1,0:T(8,128)} %copy-done.122) | copy-start | bytes 772
  302.6 9.3 %copy-start.76 = (f32[8,8]{1,0:T(8,128)S(1)}, f32[8,8]{1,0:T(8,128)}, u32[]{:S(2)}) copy-start(f32[8,8]{1,0:T(8,128)} %copy-done.75) | copy-start | bytes 772
  302.6 9.6 %copy-start.137 = (f32[8,8]{1,0:T(8,128)S(1)}, f32[8,8]{1,0:T(8,128)}, u32[]{:S(2)}) copy-start(f32[8,8]{1,0:T(8,128)} %copy-done.136) | copy-start | bytes 772
  302.6 9.6 %copy-start.99 = (f32[8,8]{1,0:T(8,128)S(1)}, f32[8,8]{1,0:T(8,128)}, u32[]{:S(2)}) copy-start(f32[8,8]{1,0:T(8,128)} %copy-done.98) | copy-start | bytes 772
  308.6 12.5 %copy-start.26 = (bf16[2048,256]{1,0:T(8,128)(2,1)}, bf16[2048,256]{1,0:T(8,128)(2,1)S(1)}, u32[]{:S(2)}) copy-start(bf16[2048,256]{1,0:T(8,128)(2,1)S(1)} %reshape.620) | copy-start | bytes 3145732
  310.8 9.5 %copy-start.67 = (bf16[512,256]{1,0:T(8,128)(2,1)S(1)}, bf16[512,256]{1,0:T(8,128)(2,1)}, u32[]{:S(2)}) copy-start(bf16[512,256]{1,0:T(8,128)(2,1)} %param.20) | copy-start | bytes 786436
  325.1 136.3 %all-reduce.8.cloned.1.call-start = ((), (), s32[]{:S(2)}) async-start(), calls=%async_computation.6 | async-start | bytes 4194304 | tf_op jit(solution)/shard_map/psum | solution.py:270
  334.7 325.6 %all-reduce.6.cloned.1.call-start = ((), (), s32[]{:S(2)}) async-start(), calls=%async_computation.5 | async-start | bytes 18874368 | tf_op jit(solution)/shard_map/psum | solution.py:275
  340.2 7.4 %copy-start.54 = (bf16[512,512]{1,0:T(8,128)(2,1)S(1)}, bf16[512,512]{1,0:T(8,128)(2,1)}, u32[]{:S(2)}) copy-start(bf16[512,512]{1,0:T(8,128)(2,1)} %param.23) | copy-start | bytes 1572868
  346.5 12.2 %copy-start.72 = (f32[1024]{0:T(1024)S(1)}, f32[1024]{0:T(1024)}, u32[]{:S(2)}) copy-start(f32[1024]{0:T(1024)} %copy-done.71) | copy-start | bytes 12292
  346.5 12.2 %copy-start.148 = (f32[512]{0:T(512)S(1)}, f32[512]{0:T(512)}, u32[]{:S(2)}) copy-start(f32[512]{0:T(512)} %param.17) | copy-start | bytes 6148
  347.6 11.1 %dynamic-slice-start = ((f32[2048]{0:T(1024)}, s32[]{:T(128)}), f32[1024]{0:T(1024)S(1)}, s32[]{:S(2)}) async-start(f32[2048]{0:T(1024)} %copy-done.149, s32[]{:T(128)} %select_n.28), calls=%async_computation.7 | async-start | bytes 8704 | tf_op jit(solution)/shard_map/dynamic_slice | solution.py:267
  359.4 43.9 %copy-start.9 = (f32[1024,512]{1,0:T(8,128)S(1)}, f32[1024,512]{1,0:T(8,128)}, u32[]{:S(2)}) copy-start(f32[1024,512]{1,0:T(8,128)} %copy-done.8) | copy-start | bytes 6291460
  660.3 9.9 %copy-start.37 = (f32[512,2048]{1,0:T(8,128)S(1)}, f32[512,2048]{1,0:T(8,128)}, u32[]{:S(2)}) copy-start(f32[512,2048]{1,0:T(8,128)} %get-tuple-element.128) | copy-start | bytes 12582916
  (103 other events, 276.8 us)
Sparse Core Ops, SparseCore 0:
  13.4 35.8 all-gather.1
  115.5 31.8 reduce-scatter.2
  325.2 32.8 reduce-scatter.4
  362.6 98.8 all-reduce.7
  469.0 191.2 all-reduce.5
